TPU v7x, 128 devices: a whole 4x4x4 slice. The times are simulated.
128 devices in a mesh: subj: 8 (over x, y_lo), slab: 16 (over y_hi, z, core).
Axes of the slice: x: 4, y: 4 (y_hi: 2, y_lo: 2; y = y_hi * 2 + y_lo), z: 4, core: 2. Of those that a mesh axis runs over, the one named last changes fastest.
Arguments:
- subjects: float32 [16, 128, 448, 128], P('subj', 'slab'), may hold values from -8 to 8
- templates: float32 [4, 128, 448, 128], P(None, 'slab', 'subj'), may hold values from -6 to 6
- labels: int32 [16], replicated, may hold values from 0 to 3, as said below
- group_live_counts: int32 [8], replicated, may hold values from 1 to 2, as said below
Outputs:
- new_templates: float32 [4, 128, 448, 128], P(None, 'slab', 'subj')
Inputs may be any that keep to these rules, and one draw needn't show every extreme that they name: `labels`: slot j belongs to group j // 2; slot 0 of group g has label g mod 4. The live slots of group g are its first group_live_counts[g] slots; the other slots hold volumes of no subject; some group has all 2 slots live.
All inputs are finite; a program needn't handle non-finite values.
Results may differ from a plain program's by a relative error of at most 0.00002.
Values sent between devices are 32-bit elements; how exact they have to be, the bound alone decides.
No kernel may reach another device: no remote copies, remote signals or barrier semaphores. Data moves between devices by JAX's collectives and lax.ppermute only.
A program may use at most 192 MiB of HBM per device.

v0:
```python
import jax
import jax.numpy as jnp
from jax import lax
from jax.sharding import PartitionSpec as P

RADIUS = 4
epsilon = 1e-05
step_size = 0.5


def extended(block, sides, width):
    for axis, dim in sides:
        count = lax.axis_size(axis)
        forward = [(i, i + 1) for i in range(count - 1)]
        backward = [(target, source) for source, target in forward]
        low = lax.ppermute(
            lax.slice_in_dim(block, block.shape[dim] - width, None, axis=dim), axis, forward
        )
        high = lax.ppermute(lax.slice_in_dim(block, 0, width, axis=dim), axis, backward)
        block = jnp.concatenate([low, block, high], axis=dim)
    return block


def window_sum(volume, which_axis, extent):
    running = lax.slice_in_dim(volume, 0, extent, axis=which_axis)
    for offset in range(1, 2 * RADIUS + 1):
        running = running + lax.slice_in_dim(volume, offset, offset + extent, axis=which_axis)
    return running


def padded_sum(volume, which_axis):
    widths = [(0, 0)] * volume.ndim
    widths[which_axis] = (RADIUS, RADIUS)
    return window_sum(jnp.pad(volume, widths), which_axis, volume.shape[which_axis])


def plane_box(volume, leading):
    return padded_sum(padded_sum(volume, leading), leading + 1)


def similarity_gradient(subject_ext, template_ext, slab_depth, rim):
    window = float((2 * RADIUS + 1) ** 3)
    row_count = subject_ext.shape[0] - 2 * RADIUS
    channels = jnp.stack(
        [
            subject_ext,
            template_ext,
            subject_ext * subject_ext,
            template_ext * template_ext,
            subject_ext * template_ext,
        ]
    )
    local_sums = plane_box(window_sum(channels, 1, row_count), 2)
    subject_sum = local_sums[0]
    template_sum = local_sums[1]
    covariance = local_sums[4] - subject_sum * template_sum / window
    subject_variance = local_sums[2] - subject_sum * subject_sum / window
    template_variance = local_sums[3] - template_sum * template_sum / window
    denominator = subject_variance * template_variance + epsilon
    cross_weight = 2.0 * covariance / denominator
    spread_weight = -covariance * covariance * subject_variance / (denominator * denominator)
    mean_weight = -(cross_weight * subject_sum + 2.0 * spread_weight * template_sum) / window
    stacked = jnp.stack([mean_weight, cross_weight, spread_weight])
    stacked = extended(stacked, (("slab", 1),), RADIUS)
    filtered = plane_box(window_sum(stacked, 1, slab_depth), 2)
    centre_subject = subject_ext[rim : rim + slab_depth]
    centre_template = template_ext[rim : rim + slab_depth]
    return filtered[0] + filtered[1] * centre_subject + 2.0 * filtered[2] * centre_template


def per_device(subjects, templates, labels, group_live_counts):
    rim = RADIUS
    group_index = lax.axis_index("subj")
    slot_total = subjects.shape[0]
    slab_depth = subjects.shape[1]
    clusters = templates.shape[0]
    group_total = group_live_counts.shape[0]
    slot_positions = jnp.arange(labels.shape[0], dtype=jnp.int32)
    group_ids = jnp.arange(group_total, dtype=jnp.int32)
    slot_live_counts = jnp.sum(
        jnp.where(
            (slot_positions // slot_total)[:, None] == group_ids[None, :],
            group_live_counts[None, :],
            0,
        ),
        axis=1,
    )
    live_mask = (slot_positions % slot_total < slot_live_counts).astype(jnp.float32)
    cluster_membership = (labels[:, None] == jnp.arange(clusters, dtype=jnp.int32)[None, :]).astype(
        jnp.float32
    ) * live_mask[:, None]
    members = jnp.sum(cluster_membership, axis=0)
    planes = lax.all_gather(templates, "subj", axis=2, tiled=True)
    template_ext = extended(planes, (("slab", 1),), rim)
    subject_ext = extended(subjects, (("slab", 1),), rim)
    own_labels = lax.dynamic_slice_in_dim(labels, group_index * slot_total, slot_total)
    own_load = jnp.sum(jnp.where(group_ids == group_index, group_live_counts, 0))

    def accumulate(slot_number, cluster_totals):
        cluster_label = own_labels[slot_number]
        live_weight = (slot_number < own_load).astype(jnp.float32)
        subject = lax.dynamic_index_in_dim(subject_ext, slot_number, 0, keepdims=False)
        template = lax.dynamic_index_in_dim(template_ext, cluster_label, 0, keepdims=False)
        template_gradient = similarity_gradient(subject, template, slab_depth, rim)
        current = lax.dynamic_index_in_dim(cluster_totals, cluster_label, 0, keepdims=False)
        return lax.dynamic_update_index_in_dim(
            cluster_totals, current + live_weight * template_gradient, cluster_label, 0
        )

    empty = jnp.zeros((clusters, slab_depth, subjects.shape[2], subjects.shape[3]), jnp.float32)
    cluster_totals = lax.fori_loop(0, slot_total, accumulate, empty)
    summed = lax.psum_scatter(cluster_totals, "subj", scatter_dimension=2, tiled=True)
    return templates + step_size * summed / members[:, None, None, None]


def solution(mesh):
    in_specs = (P("subj", "slab", None, None), P(None, "slab", "subj", None), P(), P())
    out_specs = P(None, "slab", "subj", None)
    return jax.shard_map(
        per_device, mesh=mesh, in_specs=in_specs, out_specs=out_specs, check_vma=False
    )
```

profile of v0, /device:TPU:1, one launch (start us, length us, event | category | flops | bytes accessed | tf_op | source)
XLA Modules:
  0.0 854.7 jit_solution(321791496275400842)
XLA Ops:
  7.3 153.4 %all-gather.2.cloned.1.call-done = f32[4,8,448,128]{3,2,1,0:T(8,128)} async-done(((f32[4,8,56,128]{3,2,1,0:T(8,128)}), f32[4,8,448,128]{3,2,1,0:T(8,128)}) %all-gather.2.cloned.1.call-update) | async-done | bytes 7340048 | tf_op jit(solution)/shard_map/all_gather | solution.py:93
  160.7 7.0 fusion.33
  167.7 4.0 collective-permute-start.4
  171.8 2.3 collective-permute-start.5
  174.1 2.3 fusion.34
  176.3 3.2 collective-permute-start.2
  182.2 49.3 %collective-permute-done.2 = f32[2,4,448,128]{3,2,1,0:T(8,128)S(1)} collective-permute-done((f32[2,4,448,128]{3,2,1,0:T(8,128)}, f32[2,4,448,128]{3,2,1,0:T(8,128)S(1)}, u32[]{:S(2)}, u32[]{:S(2)}) %collective-permute-start.2) | collective-permute-done | bytes 1835040 | tf_op jit(solution)/shard_map/ppermute | solution.py:16
  231.5 4.4 collective-permute-done.3
  235.9 5.1 pad_maximum_fusion.3
  241.0 8.7 %pad_maximum_fusion.2 = f32[4,16,448,128]{3,2,1,0:T(8,128)} fusion(f32[4,4,448,128]{3,2,1,0:T(8,128)} %collective-permute-done.5, f32[4,8,448,128]{3,2,1,0:T(8,128)S(1)} %bitcast.4, f32[4,4,448,128]{3,2,1,0:T(8,128)} %collective-permute-done.4), kind=kLoop, calls=%fused_computation.86 | loop fusion | flops 7340032 | bytes 29360128 | tf_op jit(solution)/shard_map/concatenate | solution.py:20
  249.7 3.9 broadcast_in_dim.30
  253.6 429.4 %while.15 = (s32[]{:T(128)}, f32[4,8,448,128]{3,2,1,0:T(8,128)}, s32[2]{0:T(128)S(1)}, s32[]{:T(128)}, f32[2,16,448,128]{3,2,1,0:T(8,128)}, /*index=5*/f32[4,16,...) while((s32[]{:T(128)}, f32[4,8,448,128]{3,2,1,0:T(8,128)}, s32[2]{0:T(128)S(1)}, s32[]{:T(128)}, ...), condition=%wide.region_2.3_spmd, body=%wide.region_1.2_spmd.sunk | while | flops 122945536 | bytes 389022016 | solution.py:111
  255.5 4.2 dynamic-slice_dynamic-update-slice_fusion.4
  260.3 4.4 dynamic-slice_dynamic-update-slice_fusion.5
  265.8 2.3 multiply_dynamic-update-slice_fusion.6
  268.2 4.3 multiply_dynamic-update-slice_fusion.7
  272.4 4.4 multiply_dynamic-update-slice_fusion.8
  276.9 27.5 %slice_add_fusion.21 = f32[5,8,448,128]{3,2,1,0:T(8,128)S(1)} fusion(f32[5,16,448,128]{3,2,1,0:T(8,128)} %multiply_dynamic-update-slice_fusion.8), kind=kLoop, calls=%fused_computation.24.clone.1 | loop fusion | flops 18350080 | bytes 91750400 | tf_op jit(solution)/shard_map/while/body/eval_jaxpr/add | solution.py:27
  304.3 8.6 %slice_add_fusion.22 = f32[5,8,448,128]{3,2,1,0:T(8,128)} fusion(f32[5,8,448,128]{3,2,1,0:T(8,128)S(1)} %slice_add_fusion.21), kind=kLoop, calls=%fused_computation.32.clone.1 | loop fusion | flops 18350080 | bytes 18350080 | tf_op jit(solution)/shard_map/while/body/eval_jaxpr/add | solution.py:27
  312.9 33.1 %fusion.39 = f32[5,8,448,128]{3,2,1,0:T(8,128)S(1)} fusion(f32[5,8,448,128]{3,2,1,0:T(8,128)} %slice_add_fusion.22), kind=kLoop, calls=%fused_computation.23.clone.1 | loop fusion | flops 18350080 | bytes 18350080 | tf_op jit(solution)/shard_map/while/body/eval_jaxpr/add | solution.py:27
  349.5 2.9 fusion.40
  354.3 3.9 collective-permute-start.1
  358.8 25.8 %collective-permute-done = f32[3,4,448,128]{3,2,1,0:T(8,128)} collective-permute-done((f32[3,4,448,128]{3,2,1,0:T(8,128)}, f32[3,4,448,128]{3,2,1,0:T(8,128)}, u32[]{:S(2)}, u32[]{:S(2)}) %collective-permute-start) | collective-permute-done | bytes 2752544 | tf_op jit(solution)/shard_map/while/body/eval_jaxpr/ppermute | solution.py:16
  384.6 4.4 collective-permute-done.1
  389.0 9.3 %maximum_maximum_fusion.2 = (f32[3,12,448,128]{3,2,1,0:T(8,128)}, f32[3,12,448,128]{3,2,1,0:T(8,128)}) fusion(f32[1,8,448,128]{3,2,1,0:T(8,128)} %copy-done.1, f32[1,8,448,128]{3,2,1,0:T(8,128)} %copy-done, f32[1,8,448,128]{3,2,1,0:T(8,128)S(1)} %get-tuple-element.229, f32[3,4,448,128]{3,2,1,0:T(8,128)} %collective-permute-done, ...), kind=kLoop, calls=%fused_computation.38.clone.1 | loop fusion | flops 12386304 | bytes 27525120 | tf_op jit(solution)/shard_map/while/body/eval_jaxpr/concatenate | solution.py:20
  398.3 19.3 %slice_add_fusion.23 = f32[3,8,448,128]{3,2,1,0:T(8,128)} fusion(f32[3,12,448,128]{3,2,1,0:T(8,128)} %get-tuple-element.232, f32[3,12,448,128]{3,2,1,0:T(8,128)} %get-tuple-element.233, f32[1,8,448,128]{3,2,1,0:T(8,128)} %copy-done.1, f32[1,8,448,128]{3,2,1,0:T(8,128)} %copy-done, f32[1,8,448,128]{3,2,1,0:T(8,128)S(1)} %get-tuple-element.229), kind=kLoop, calls=%fused_computation.48.clone.1 | loop fusion | flops 13762560 | bytes 55050240 | tf_op jit(solution)/shard_map/while/body/eval_jaxpr/add | solution.py:27
  417.6 20.5 %slice_add_fusion.24 = f32[3,8,448,128]{3,2,1,0:T(8,128)} fusion(f32[3,8,448,128]{3,2,1,0:T(8,128)} %slice_add_fusion.23), kind=kLoop, calls=%fused_computation.57.clone.1 | loop fusion | flops 11010048 | bytes 11010048 | tf_op jit(solution)/shard_map/while/body/eval_jaxpr/add | solution.py:27
  438.1 24.2 %fusion.41 = f32[3,8,448,128]{3,2,1,0:T(8,128)} fusion(f32[3,8,448,128]{3,2,1,0:T(8,128)} %slice_add_fusion.24), kind=kLoop, calls=%fused_computation.47.clone.1 | loop fusion | flops 11010048 | bytes 11010048 | tf_op jit(solution)/shard_map/while/body/eval_jaxpr/add | solution.py:27
  462.2 6.1 fusion.42
  470.2 4.2 dynamic-slice_dynamic-update-slice_fusion.4
  475.1 4.4 dynamic-slice_dynamic-update-slice_fusion.5
  480.6 2.3 multiply_dynamic-update-slice_fusion.6
  482.9 4.3 multiply_dynamic-update-slice_fusion.7
  487.2 4.4 multiply_dynamic-update-slice_fusion.8
  491.6 27.5 %slice_add_fusion.21 = f32[5,8,448,128]{3,2,1,0:T(8,128)S(1)} fusion(f32[5,16,448,128]{3,2,1,0:T(8,128)} %multiply_dynamic-update-slice_fusion.8), kind=kLoop, calls=%fused_computation.24.clone.1 | loop fusion | flops 18350080 | bytes 91750400 | tf_op jit(solution)/shard_map/while/body/eval_jaxpr/add | solution.py:27
  519.1 8.6 %slice_add_fusion.22 = f32[5,8,448,128]{3,2,1,0:T(8,128)} fusion(f32[5,8,448,128]{3,2,1,0:T(8,128)S(1)} %slice_add_fusion.21), kind=kLoop, calls=%fused_computation.32.clone.1 | loop fusion | flops 18350080 | bytes 18350080 | tf_op jit(solution)/shard_map/while/body/eval_jaxpr/add | solution.py:27
  527.7 33.1 %fusion.39 = f32[5,8,448,128]{3,2,1,0:T(8,128)S(1)} fusion(f32[5,8,448,128]{3,2,1,0:T(8,128)} %slice_add_fusion.22), kind=kLoop, calls=%fused_computation.23.clone.1 | loop fusion | flops 18350080 | bytes 18350080 | tf_op jit(solution)/shard_map/while/body/eval_jaxpr/add | solution.py:27
  564.2 2.9 fusion.40
  569.1 3.9 collective-permute-start.1
  573.6 25.8 %collective-permute-done = f32[3,4,448,128]{3,2,1,0:T(8,128)} collective-permute-done((f32[3,4,448,128]{3,2,1,0:T(8,128)}, f32[3,4,448,128]{3,2,1,0:T(8,128)}, u32[]{:S(2)}, u32[]{:S(2)}) %collective-permute-start) | collective-permute-done | bytes 2752544 | tf_op jit(solution)/shard_map/while/body/eval_jaxpr/ppermute | solution.py:16
  599.4 4.4 collective-permute-done.1
  603.8 9.3 %maximum_maximum_fusion.2 = (f32[3,12,448,128]{3,2,1,0:T(8,128)}, f32[3,12,448,128]{3,2,1,0:T(8,128)}) fusion(f32[1,8,448,128]{3,2,1,0:T(8,128)} %copy-done.1, f32[1,8,448,128]{3,2,1,0:T(8,128)} %copy-done, f32[1,8,448,128]{3,2,1,0:T(8,128)S(1)} %get-tuple-element.229, f32[3,4,448,128]{3,2,1,0:T(8,128)} %collective-permute-done, ...), kind=kLoop, calls=%fused_computation.38.clone.1 | loop fusion | flops 12386304 | bytes 27525120 | tf_op jit(solution)/shard_map/while/body/eval_jaxpr/concatenate | solution.py:20
  613.1 19.3 %slice_add_fusion.23 = f32[3,8,448,128]{3,2,1,0:T(8,128)} fusion(f32[3,12,448,128]{3,2,1,0:T(8,128)} %get-tuple-element.232, f32[3,12,448,128]{3,2,1,0:T(8,128)} %get-tuple-element.233, f32[1,8,448,128]{3,2,1,0:T(8,128)} %copy-done.1, f32[1,8,448,128]{3,2,1,0:T(8,128)} %copy-done, f32[1,8,448,128]{3,2,1,0:T(8,128)S(1)} %get-tuple-element.229), kind=kLoop, calls=%fused_computation.48.clone.1 | loop fusion | flops 13762560 | bytes 55050240 | tf_op jit(solution)/shard_map/while/body/eval_jaxpr/add | solution.py:27
  632.3 20.5 %slice_add_fusion.24 = f32[3,8,448,128]{3,2,1,0:T(8,128)} fusion(f32[3,8,448,128]{3,2,1,0:T(8,128)} %slice_add_fusion.23), kind=kLoop, calls=%fused_computation.57.clone.1 | loop fusion | flops 11010048 | bytes 11010048 | tf_op jit(solution)/shard_map/while/body/eval_jaxpr/add | solution.py:27
  652.8 24.2 %fusion.41 = f32[3,8,448,128]{3,2,1,0:T(8,128)} fusion(f32[3,8,448,128]{3,2,1,0:T(8,128)} %slice_add_fusion.24), kind=kLoop, calls=%fused_computation.47.clone.1 | loop fusion | flops 11010048 | bytes 11010048 | tf_op jit(solution)/shard_map/while/body/eval_jaxpr/add | solution.py:27
  677.0 6.1 fusion.42
  683.9 161.7 %reduce-scatter.2.cloned.1.call-done = f32[4,8,56,128]{3,2,1,0:T(8,128)} async-done(((f32[4,8,448,128]{3,2,1,0:T(8,128)}), f32[4,8,56,128]{3,2,1,0:T(8,128)}) %reduce-scatter.2.cloned.1.call-update) | async-done | bytes 917520 | tf_op jit(solution)/shard_map/reduce_scatter | solution.py:112
  845.6 2.3 divide_add_fusion
  (50 shorter events, 18.1 us)
Async XLA Ops:
  6.5 154.2 %all-gather.2.cloned.1.call-start = ((), (), s32[]{:S(2)}) async-start(), calls=%async_computation.1 | async-start | bytes 8257536 | tf_op jit(solution)/shard_map/all_gather | solution.py:93
  7.3 838.3 %reduce-scatter.2.cloned.1.call-start = ((), (), s32[]{:S(2)}) async-start(), calls=%async_computation.2 | async-start | bytes 8257536 | tf_op jit(solution)/shard_map/reduce_scatter | solution.py:112
  160.7 13.4 %copy-start.3 = (f32[2,8,448,128]{3,2,1,0:T(8,128)S(1)}, f32[2,8,448,128]{3,2,1,0:T(8,128)}, u32[]{:S(2)}) copy-start(f32[2,8,448,128]{3,2,1,0:T(8,128)} %param.6) | copy-start | bytes 11010052
  167.7 13.8 %copy-start.7 = (s32[16]{0:T(128)S(1)}, s32[16]{0:T(128)}, u32[]{:S(2)}) copy-start(s32[16]{0:T(128)} %param.8) | copy-start | bytes 196
  167.7 13.9 %copy-start.5 = (s32[8]{0:T(128)S(1)}, s32[8]{0:T(128)}, u32[]{:S(2)}) copy-start(s32[8]{0:T(128)} %param.9) | copy-start | bytes 100
  167.7 73.3 %collective-permute-start.4 = (f32[4,4,448,128]{3,2,1,0:T(8,128)}, f32[4,4,448,128]{3,2,1,0:T(8,128)}, u32[]{:S(2)}, u32[]{:S(2)}) collective-permute-start(f32[4,4,448,128]{3,2,1,0:T(8,128)} %get-tuple-element.179), channel_id=1, source_target_pairs={{0,1},{1,2},{2,3},{3,4},{4,5},{5,6},{6,7},{7,8},{8,9},{9,10},{10,1... | collective-permute-start | bytes 11010056 | tf_op jit(solution)/shard_map/ppermute | solution.py:16
  171.8 69.3 %collective-permute-start.5 = (f32[4,4,448,128]{3,2,1,0:T(8,128)}, f32[4,4,448,128]{3,2,1,0:T(8,128)}, u32[]{:S(2)}, u32[]{:S(2)}) collective-permute-start(f32[4,4,448,128]{3,2,1,0:T(8,128)} %get-tuple-element.180), channel_id=1, source_target_pairs={{1,0},{2,1},{3,2},{4,3},{5,4},{6,5},{7,6},{8,7},{9,8},{10,9},{11,1... | collective-permute-start | bytes 11010056 | tf_op jit(solution)/shard_map/ppermute | solution.py:19
  176.3 55.2 %collective-permute-start.2 = (f32[2,4,448,128]{3,2,1,0:T(8,128)}, f32[2,4,448,128]{3,2,1,0:T(8,128)S(1)}, u32[]{:S(2)}, u32[]{:S(2)}) collective-permute-start(f32[2,4,448,128]{3,2,1,0:T(8,128)} %get-tuple-element.181), channel_id=1, source_target_pairs={{0,1},{1,2},{2,3},{3,4},{4,5},{5,6},{6,7},{7,8},{8,9},{9,10},{10,1... | collective-permute-start | bytes 5505032 | tf_op jit(solution)/shard_map/ppermute | solution.py:16
  179.6 56.4 %collective-permute-start.3 = (f32[2,4,448,128]{3,2,1,0:T(8,128)}, f32[2,4,448,128]{3,2,1,0:T(8,128)}, u32[]{:S(2)}, u32[]{:S(2)}) collective-permute-start(f32[2,4,448,128]{3,2,1,0:T(8,128)} %get-tuple-element.182), channel_id=1, source_target_pairs={{1,0},{2,1},{3,2},{4,3},{5,4},{6,5},{7,6},{8,7},{9,8},{10,9},{11,1... | collective-permute-start | bytes 5505032 | tf_op jit(solution)/shard_map/ppermute | solution.py:19
  181.6 59.4 %slice-start = ((s8[7340032]{0:T(1024)(128)(4,1)}), s8[4194304]{0:T(1024)(128)(4,1)S(1)}, s32[]{:S(2)}) async-start(s8[7340032]{0:T(1024)(128)(4,1)} %bitcast.3), calls=%async_computation.3 | async-start | bytes 8388608
  182.2 58.8 %slice-start.1 = ((s8[7340032]{0:T(1024)(128)(4,1)}), s8[3145728]{0:T(1024)(128)(4,1)S(1)}, s32[]{:S(2)}) async-start(s8[7340032]{0:T(1024)(128)(4,1)} %bitcast.3), calls=%async_computation.4 | async-start | bytes 6291456
  260.3 5.5 copy-start.2
  347.6 1.3 copy-start
  347.7 1.8 copy-start.1
  352.4 32.2 %collective-permute-start = (f32[3,4,448,128]{3,2,1,0:T(8,128)}, f32[3,4,448,128]{3,2,1,0:T(8,128)}, u32[]{:S(2)}, u32[]{:S(2)}) collective-permute-start(f32[3,4,448,128]{3,2,1,0:T(8,128)} %get-tuple-element.230), channel_id=1, source_target_pairs={{0,1},{1,2},{2,3},{3,4},{4,5},{5,6},{6,7},{7,8},{8,9},{9,10},{10,1... | collective-permute-start | bytes 8257544 | tf_op jit(solution)/shard_map/while/body/eval_jaxpr/ppermute | solution.py:16
  354.3 34.7 %collective-permute-start.1 = (f32[3,4,448,128]{3,2,1,0:T(8,128)}, f32[3,4,448,128]{3,2,1,0:T(8,128)}, u32[]{:S(2)}, u32[]{:S(2)}) collective-permute-start(f32[3,4,448,128]{3,2,1,0:T(8,128)} %get-tuple-element.231), channel_id=1, source_target_pairs={{1,0},{2,1},{3,2},{4,3},{5,4},{6,5},{7,6},{8,7},{9,8},{10,9},{11,1... | collective-permute-start | bytes 8257544 | tf_op jit(solution)/shard_map/while/body/eval_jaxpr/ppermute | solution.py:19
  475.1 5.5 copy-start.2
  562.4 1.3 copy-start
  562.4 1.8 copy-start.1
  567.2 32.2 %collective-permute-start = (f32[3,4,448,128]{3,2,1,0:T(8,128)}, f32[3,4,448,128]{3,2,1,0:T(8,128)}, u32[]{:S(2)}, u32[]{:S(2)}) collective-permute-start(f32[3,4,448,128]{3,2,1,0:T(8,128)} %get-tuple-element.230), channel_id=1, source_target_pairs={{0,1},{1,2},{2,3},{3,4},{4,5},{5,6},{6,7},{7,8},{8,9},{9,10},{10,1... | collective-permute-start | bytes 8257544 | tf_op jit(solution)/shard_map/while/body/eval_jaxpr/ppermute | solution.py:16
  569.1 34.7 %collective-permute-start.1 = (f32[3,4,448,128]{3,2,1,0:T(8,128)}, f32[3,4,448,128]{3,2,1,0:T(8,128)}, u32[]{:S(2)}, u32[]{:S(2)}) collective-permute-start(f32[3,4,448,128]{3,2,1,0:T(8,128)} %get-tuple-element.231), channel_id=1, source_target_pairs={{1,0},{2,1},{3,2},{4,3},{5,4},{6,5},{7,6},{8,7},{9,8},{10,9},{11,1... | collective-permute-start | bytes 8257544 | tf_op jit(solution)/shard_map/while/body/eval_jaxpr/ppermute | solution.py:19
  683.0 0.7 copy-start.6
  683.0 0.7 copy-start.8
  683.0 162.6 %copy-start.4 = (f32[4,8,56,128]{3,2,1,0:T(8,128)S(1)}, f32[4,8,56,128]{3,2,1,0:T(8,128)}, u32[]{:S(2)}) copy-start(f32[4,8,56,128]{3,2,1,0:T(8,128)} %param.7) | copy-start | bytes 2752516
Sparse Core Ops, SparseCore 0:
  9.0 151.6 all-gather.1
  683.2 162.3 reduce-scatter.1
where the time goes:
time: 855 us
  waiting for transfers between devices  430 us (50%)
  other arithmetic  340 us (40%)
  local copies, waits for them, and re-layouts  43 us (5%)
  starting transfers between devices  23.2 us (3%)
  between operations  13.5 us (2%)
    add x12, other arithmetic, window_sum(): running + lax.slice_in_dim(volume, offset, offset + extent, axis=which_axis)  266 us
    reduce_scatter x1, waiting for transfers between devices, per_device(): lax.psum_scatter(cluster_totals, 'subj', scatter_dimension=2, tiled=True)  162 us
    all_gather x1, waiting for transfers between devices, per_device(): planes = lax.all_gather(templates, 'subj', axis=2, tiled=True)  153 us
    ppermute x4, waiting for transfers between devices, extended(): lax.ppermute(lax.slice_in_dim(block, block.shape[dim] - width, None, axis...  101 us
    concatenate x4, other arithmetic, extended(): block = jnp.concatenate([low, block, high], axis=dim)  32.3 us
    while x16, local copies, waits for them, and re-layouts  22 us
  transfers between devices with their start and end apart: 10, of which 8 were waited for; matrix products, arithmetic and copies ran while one was open for 1% of the time, Pallas kernels for 0%

commit v1 on v0

--- a/solution.py
+++ b/solution.py
@@ -90,7 +90,9 @@
         jnp.float32
     ) * live_mask[:, None]
     members = jnp.sum(cluster_membership, axis=0)
-    planes = lax.all_gather(templates, "subj", axis=2, tiled=True)
+    planes = jnp.concatenate(
+        lax.all_to_all(jnp.stack([templates] * lax.axis_size("subj")), "subj", 0, 0), axis=2
+    )
     template_ext = extended(planes, (("slab", 1),), rim)
     subject_ext = extended(subjects, (("slab", 1),), rim)
     own_labels = lax.dynamic_slice_in_dim(labels, group_index * slot_total, slot_total)

time: 855 us -> 789 us (0.923)
  waiting for transfers between devices: 430 us -> 271 us
  blocking collectives: 0 us -> 88.4 us
    all_gather x1 -> x0, waiting for transfers between devices: 153 us -> none  [per_device(): planes = lax.all_gather(templates, 'subj', axis=2, tiled=True)]
    all_to_all x0 -> x1, blocking collectives: none -> 88.4 us  [per_device(): lax.all_to_all(jnp.stack([templates] * lax.axis_size('subj')), 'subj', 0, 0)]
  transfers between devices with their start and end apart: 10 -> 9, of which waited for: 8 -> 7; matrix products, arithmetic and copies ran while one was open for 1% -> 1% of each run, Pallas kernels for 0% -> 0%
where the time goes in v1:
time: 789 us; the launch traced here: 788 us
  other arithmetic  340 us (43%)
  waiting for transfers between devices  271 us (34%)
  blocking collectives  88.4 us (11%)
  local copies, waits for them, and re-layouts  44.9 us (6%)
  starting transfers between devices  24.5 us (3%)
  between operations  13.5 us (2%)
    add x12, other arithmetic, window_sum(): running + lax.slice_in_dim(volume, offset, offset + extent, axis=which_axis)  266 us
    reduce_scatter x1, waiting for transfers between devices, per_device(): lax.psum_scatter(cluster_totals, 'subj', scatter_dimension=2, tiled=True)  157 us
    ppermute x4, waiting for transfers between devices, extended(): lax.ppermute(lax.slice_in_dim(block, block.shape[dim] - width, None, axis...  101 us
    all_to_all x1, blocking collectives, per_device(): lax.all_to_all(jnp.stack([templates] * lax.axis_size('subj')), 'subj', 0, 0)  88.4 us
    concatenate x4, other arithmetic, extended(): block = jnp.concatenate([low, block, high], axis=dim)  32.9 us
    while x16, local copies, waits for them, and re-layouts  22.1 us
  transfers between devices with their start and end apart: 9, of which 7 were waited for; matrix products, arithmetic and copies ran while one was open for 1% of the time, Pallas kernels for 0%

profile of v1, /device:TPU:1, one launch (start us, length us, event | category | flops | bytes accessed | tf_op | source)
XLA Modules:
  0.0 788.0 jit_solution(1646639253835451657)
XLA Ops:
  6.5 2.0 stack.51
  8.6 88.4 %all_to_all.5 = f32[8,4,8,56,128]{4,3,2,1,0:T(8,128)S(1)} all-to-all(f32[8,4,8,56,128]{4,3,2,1,0:T(8,128)S(1)} %stack.51), channel_id=1, replica_groups=mesh['subj'=8,'slab'=16] {'subj'}, dimensions={0} | all-to-all | bytes 14680064 | tf_op jit(solution)/shard_map/all_to_all | solution.py:94
  98.0 4.1 fusion.33
  103.9 5.4 collective-permute-start.4
  111.2 2.2 fusion.34
  113.5 3.6 collective-permute-start.2
  119.8 49.3 %collective-permute-done.2 = f32[2,4,448,128]{3,2,1,0:T(8,128)S(1)} collective-permute-done((f32[2,4,448,128]{3,2,1,0:T(8,128)}, f32[2,4,448,128]{3,2,1,0:T(8,128)S(1)}, u32[]{:S(2)}, u32[]{:S(2)}) %collective-permute-start.2) | collective-permute-done | bytes 1835040 | tf_op jit(solution)/shard_map/ppermute | solution.py:16
  169.1 4.4 collective-permute-done.3
  173.5 5.1 pad_maximum_fusion.3
  178.6 8.7 %pad_maximum_fusion.2 = f32[4,16,448,128]{3,2,1,0:T(8,128)} fusion(f32[4,4,448,128]{3,2,1,0:T(8,128)} %collective-permute-done.5, f32[4,8,448,128]{3,2,1,0:T(8,128)S(1)} %bitcast.9, f32[4,4,448,128]{3,2,1,0:T(8,128)} %collective-permute-done.4), kind=kLoop, calls=%fused_computation.86 | loop fusion | flops 7340032 | bytes 29360128 | tf_op jit(solution)/shard_map/concatenate | solution.py:20
  187.3 3.9 broadcast_in_dim.30
  191.2 429.9 %while.15 = (s32[]{:T(128)}, f32[4,8,448,128]{3,2,1,0:T(8,128)}, s32[2]{0:T(128)S(1)}, s32[]{:T(128)}, f32[2,16,448,128]{3,2,1,0:T(8,128)}, /*index=5*/f32[4,16,...) while((s32[]{:T(128)}, f32[4,8,448,128]{3,2,1,0:T(8,128)}, s32[2]{0:T(128)S(1)}, s32[]{:T(128)}, ...), condition=%wide.region_2.3_spmd, body=%wide.region_1.2_spmd.sunk | while | flops 122945536 | bytes 389022016 | solution.py:113
  193.0 4.2 dynamic-slice_dynamic-update-slice_fusion.4
  197.9 4.4 dynamic-slice_dynamic-update-slice_fusion.5
  203.4 2.3 multiply_dynamic-update-slice_fusion.6
  205.7 4.3 multiply_dynamic-update-slice_fusion.7
  210.0 4.4 multiply_dynamic-update-slice_fusion.8
  214.4 27.3 %slice_add_fusion.21 = f32[5,8,448,128]{3,2,1,0:T(8,128)S(1)} fusion(f32[5,16,448,128]{3,2,1,0:T(8,128)} %multiply_dynamic-update-slice_fusion.8), kind=kLoop, calls=%fused_computation.24.clone.1 | loop fusion | flops 18350080 | bytes 91750400 | tf_op jit(solution)/shard_map/while/body/eval_jaxpr/add | solution.py:27
  241.7 8.6 %slice_add_fusion.22 = f32[5,8,448,128]{3,2,1,0:T(8,128)} fusion(f32[5,8,448,128]{3,2,1,0:T(8,128)S(1)} %slice_add_fusion.21), kind=kLoop, calls=%fused_computation.32.clone.1 | loop fusion | flops 18350080 | bytes 18350080 | tf_op jit(solution)/shard_map/while/body/eval_jaxpr/add | solution.py:27
  250.4 33.1 %fusion.39 = f32[5,8,448,128]{3,2,1,0:T(8,128)S(1)} fusion(f32[5,8,448,128]{3,2,1,0:T(8,128)} %slice_add_fusion.22), kind=kLoop, calls=%fused_computation.23.clone.1 | loop fusion | flops 18350080 | bytes 18350080 | tf_op jit(solution)/shard_map/while/body/eval_jaxpr/add | solution.py:27
  286.9 2.9 fusion.40
  291.8 3.9 collective-permute-start.1
  296.3 25.8 %collective-permute-done = f32[3,4,448,128]{3,2,1,0:T(8,128)} collective-permute-done((f32[3,4,448,128]{3,2,1,0:T(8,128)}, f32[3,4,448,128]{3,2,1,0:T(8,128)}, u32[]{:S(2)}, u32[]{:S(2)}) %collective-permute-start) | collective-permute-done | bytes 2752544 | tf_op jit(solution)/shard_map/while/body/eval_jaxpr/ppermute | solution.py:16
  322.1 4.7 collective-permute-done.1
  326.8 9.6 %maximum_maximum_fusion.2 = (f32[3,12,448,128]{3,2,1,0:T(8,128)}, f32[3,12,448,128]{3,2,1,0:T(8,128)}) fusion(f32[1,8,448,128]{3,2,1,0:T(8,128)} %copy-done.1, f32[1,8,448,128]{3,2,1,0:T(8,128)} %copy-done, f32[1,8,448,128]{3,2,1,0:T(8,128)S(1)} %get-tuple-element.229, f32[3,4,448,128]{3,2,1,0:T(8,128)} %collective-permute-done, ...), kind=kLoop, calls=%fused_computation.38.clone.1 | loop fusion | flops 12386304 | bytes 27525120 | tf_op jit(solution)/shard_map/while/body/eval_jaxpr/concatenate | solution.py:20
  336.3 19.3 %slice_add_fusion.23 = f32[3,8,448,128]{3,2,1,0:T(8,128)} fusion(f32[3,12,448,128]{3,2,1,0:T(8,128)} %get-tuple-element.232, f32[3,12,448,128]{3,2,1,0:T(8,128)} %get-tuple-element.233, f32[1,8,448,128]{3,2,1,0:T(8,128)} %copy-done.1, f32[1,8,448,128]{3,2,1,0:T(8,128)} %copy-done, f32[1,8,448,128]{3,2,1,0:T(8,128)S(1)} %get-tuple-element.229), kind=kLoop, calls=%fused_computation.48.clone.1 | loop fusion | flops 13762560 | bytes 55050240 | tf_op jit(solution)/shard_map/while/body/eval_jaxpr/add | solution.py:27
  355.6 20.4 %slice_add_fusion.24 = f32[3,8,448,128]{3,2,1,0:T(8,128)} fusion(f32[3,8,448,128]{3,2,1,0:T(8,128)} %slice_add_fusion.23), kind=kLoop, calls=%fused_computation.57.clone.1 | loop fusion | flops 11010048 | bytes 11010048 | tf_op jit(solution)/shard_map/while/body/eval_jaxpr/add | solution.py:27
  376.0 24.2 %fusion.41 = f32[3,8,448,128]{3,2,1,0:T(8,128)} fusion(f32[3,8,448,128]{3,2,1,0:T(8,128)} %slice_add_fusion.24), kind=kLoop, calls=%fused_computation.47.clone.1 | loop fusion | flops 11010048 | bytes 11010048 | tf_op jit(solution)/shard_map/while/body/eval_jaxpr/add | solution.py:27
  400.2 6.1 fusion.42
  408.2 4.2 dynamic-slice_dynamic-update-slice_fusion.4
  413.1 4.4 dynamic-slice_dynamic-update-slice_fusion.5
  418.6 2.3 multiply_dynamic-update-slice_fusion.6
  420.9 4.3 multiply_dynamic-update-slice_fusion.7
  425.1 4.4 multiply_dynamic-update-slice_fusion.8
  429.6 27.3 %slice_add_fusion.21 = f32[5,8,448,128]{3,2,1,0:T(8,128)S(1)} fusion(f32[5,16,448,128]{3,2,1,0:T(8,128)} %multiply_dynamic-update-slice_fusion.8), kind=kLoop, calls=%fused_computation.24.clone.1 | loop fusion | flops 18350080 | bytes 91750400 | tf_op jit(solution)/shard_map/while/body/eval_jaxpr/add | solution.py:27
  456.9 8.6 %slice_add_fusion.22 = f32[5,8,448,128]{3,2,1,0:T(8,128)} fusion(f32[5,8,448,128]{3,2,1,0:T(8,128)S(1)} %slice_add_fusion.21), kind=kLoop, calls=%fused_computation.32.clone.1 | loop fusion | flops 18350080 | bytes 18350080 | tf_op jit(solution)/shard_map/while/body/eval_jaxpr/add | solution.py:27
  465.5 33.1 %fusion.39 = f32[5,8,448,128]{3,2,1,0:T(8,128)S(1)} fusion(f32[5,8,448,128]{3,2,1,0:T(8,128)} %slice_add_fusion.22), kind=kLoop, calls=%fused_computation.23.clone.1 | loop fusion | flops 18350080 | bytes 18350080 | tf_op jit(solution)/shard_map/while/body/eval_jaxpr/add | solution.py:27
  502.1 2.9 fusion.40
  506.9 3.9 collective-permute-start.1
  511.4 25.8 %collective-permute-done = f32[3,4,448,128]{3,2,1,0:T(8,128)} collective-permute-done((f32[3,4,448,128]{3,2,1,0:T(8,128)}, f32[3,4,448,128]{3,2,1,0:T(8,128)}, u32[]{:S(2)}, u32[]{:S(2)}) %collective-permute-start) | collective-permute-done | bytes 2752544 | tf_op jit(solution)/shard_map/while/body/eval_jaxpr/ppermute | solution.py:16
  537.2 4.4 collective-permute-done.1
  541.6 9.6 %maximum_maximum_fusion.2 = (f32[3,12,448,128]{3,2,1,0:T(8,128)}, f32[3,12,448,128]{3,2,1,0:T(8,128)}) fusion(f32[1,8,448,128]{3,2,1,0:T(8,128)} %copy-done.1, f32[1,8,448,128]{3,2,1,0:T(8,128)} %copy-done, f32[1,8,448,128]{3,2,1,0:T(8,128)S(1)} %get-tuple-element.229, f32[3,4,448,128]{3,2,1,0:T(8,128)} %collective-permute-done, ...), kind=kLoop, calls=%fused_computation.38.clone.1 | loop fusion | flops 12386304 | bytes 27525120 | tf_op jit(solution)/shard_map/while/body/eval_jaxpr/concatenate | solution.py:20
  551.2 19.3 %slice_add_fusion.23 = f32[3,8,448,128]{3,2,1,0:T(8,128)} fusion(f32[3,12,448,128]{3,2,1,0:T(8,128)} %get-tuple-element.232, f32[3,12,448,128]{3,2,1,0:T(8,128)} %get-tuple-element.233, f32[1,8,448,128]{3,2,1,0:T(8,128)} %copy-done.1, f32[1,8,448,128]{3,2,1,0:T(8,128)} %copy-done, f32[1,8,448,128]{3,2,1,0:T(8,128)S(1)} %get-tuple-element.229), kind=kLoop, calls=%fused_computation.48.clone.1 | loop fusion | flops 13762560 | bytes 55050240 | tf_op jit(solution)/shard_map/while/body/eval_jaxpr/add | solution.py:27
  570.5 20.4 %slice_add_fusion.24 = f32[3,8,448,128]{3,2,1,0:T(8,128)} fusion(f32[3,8,448,128]{3,2,1,0:T(8,128)} %slice_add_fusion.23), kind=kLoop, calls=%fused_computation.57.clone.1 | loop fusion | flops 11010048 | bytes 11010048 | tf_op jit(solution)/shard_map/while/body/eval_jaxpr/add | solution.py:27
  590.9 24.2 %fusion.41 = f32[3,8,448,128]{3,2,1,0:T(8,128)} fusion(f32[3,8,448,128]{3,2,1,0:T(8,128)} %slice_add_fusion.24), kind=kLoop, calls=%fused_computation.47.clone.1 | loop fusion | flops 11010048 | bytes 11010048 | tf_op jit(solution)/shard_map/while/body/eval_jaxpr/add | solution.py:27
  615.0 6.1 fusion.42
  622.0 157.0 %reduce-scatter.2.cloned.1.call-done = f32[4,8,56,128]{3,2,1,0:T(8,128)} async-done(((f32[4,8,448,128]{3,2,1,0:T(8,128)}), f32[4,8,56,128]{3,2,1,0:T(8,128)}) %reduce-scatter.2.cloned.1.call-update) | async-done | bytes 917520 | tf_op jit(solution)/shard_map/reduce_scatter | solution.py:114
  778.9 2.3 divide_add_fusion
  (52 shorter events, 22.1 us)
Async XLA Ops:
  6.5 772.4 %reduce-scatter.2.cloned.1.call-start = ((), (), s32[]{:S(2)}) async-start(), calls=%async_computation.2 | async-start | bytes 8257536 | tf_op jit(solution)/shard_map/reduce_scatter | solution.py:114
  97.9 6.0 copy-start.3
  98.0 13.3 %copy-start.4 = (f32[2,8,448,128]{3,2,1,0:T(8,128)S(1)}, f32[2,8,448,128]{3,2,1,0:T(8,128)}, u32[]{:S(2)}) copy-start(f32[2,8,448,128]{3,2,1,0:T(8,128)} %param.6) | copy-start | bytes 11010052
  103.9 15.1 %copy-start.8 = (s32[16]{0:T(128)S(1)}, s32[16]{0:T(128)}, u32[]{:S(2)}) copy-start(s32[16]{0:T(128)} %param.8) | copy-start | bytes 196
  103.9 15.2 %copy-start.6 = (s32[8]{0:T(128)S(1)}, s32[8]{0:T(128)}, u32[]{:S(2)}) copy-start(s32[8]{0:T(128)} %param.9) | copy-start | bytes 100
  103.9 74.6 %collective-permute-start.4 = (f32[4,4,448,128]{3,2,1,0:T(8,128)}, f32[4,4,448,128]{3,2,1,0:T(8,128)}, u32[]{:S(2)}, u32[]{:S(2)}) collective-permute-start(f32[4,4,448,128]{3,2,1,0:T(8,128)} %get-tuple-element.179), channel_id=1, source_target_pairs={{0,1},{1,2},{2,3},{3,4},{4,5},{5,6},{6,7},{7,8},{8,9},{9,10},{10,1... | collective-permute-start | bytes 11010056 | tf_op jit(solution)/shard_map/ppermute | solution.py:16
  109.3 69.3 %collective-permute-start.5 = (f32[4,4,448,128]{3,2,1,0:T(8,128)}, f32[4,4,448,128]{3,2,1,0:T(8,128)}, u32[]{:S(2)}, u32[]{:S(2)}) collective-permute-start(f32[4,4,448,128]{3,2,1,0:T(8,128)} %get-tuple-element.180), channel_id=1, source_target_pairs={{1,0},{2,1},{3,2},{4,3},{5,4},{6,5},{7,6},{8,7},{9,8},{10,9},{11,1... | collective-permute-start | bytes 11010056 | tf_op jit(solution)/shard_map/ppermute | solution.py:19
  113.5 55.6 %collective-permute-start.2 = (f32[2,4,448,128]{3,2,1,0:T(8,128)}, f32[2,4,448,128]{3,2,1,0:T(8,128)S(1)}, u32[]{:S(2)}, u32[]{:S(2)}) collective-permute-start(f32[2,4,448,128]{3,2,1,0:T(8,128)} %get-tuple-element.181), channel_id=1, source_target_pairs={{0,1},{1,2},{2,3},{3,4},{4,5},{5,6},{6,7},{7,8},{8,9},{9,10},{10,1... | collective-permute-start | bytes 5505032 | tf_op jit(solution)/shard_map/ppermute | solution.py:16
  117.1 56.4 %collective-permute-start.3 = (f32[2,4,448,128]{3,2,1,0:T(8,128)}, f32[2,4,448,128]{3,2,1,0:T(8,128)}, u32[]{:S(2)}, u32[]{:S(2)}) collective-permute-start(f32[2,4,448,128]{3,2,1,0:T(8,128)} %get-tuple-element.182), channel_id=1, source_target_pairs={{1,0},{2,1},{3,2},{4,3},{5,4},{6,5},{7,6},{8,7},{9,8},{10,9},{11,1... | collective-permute-start | bytes 5505032 | tf_op jit(solution)/shard_map/ppermute | solution.py:19
  119.2 59.4 %slice-start = ((s8[7340032]{0:T(1024)(128)(4,1)}), s8[4194304]{0:T(1024)(128)(4,1)S(1)}, s32[]{:S(2)}) async-start(s8[7340032]{0:T(1024)(128)(4,1)} %bitcast.7), calls=%async_computation.3 | async-start | bytes 8388608
  119.8 58.8 %slice-start.1 = ((s8[7340032]{0:T(1024)(128)(4,1)}), s8[3145728]{0:T(1024)(128)(4,1)S(1)}, s32[]{:S(2)}) async-start(s8[7340032]{0:T(1024)(128)(4,1)} %bitcast.7), calls=%async_computation.4 | async-start | bytes 6291456
  197.9 5.5 copy-start.2
  285.1 1.3 copy-start
  285.1 1.8 copy-start.1
  289.9 32.2 %collective-permute-start = (f32[3,4,448,128]{3,2,1,0:T(8,128)}, f32[3,4,448,128]{3,2,1,0:T(8,128)}, u32[]{:S(2)}, u32[]{:S(2)}) collective-permute-start(f32[3,4,448,128]{3,2,1,0:T(8,128)} %get-tuple-element.230), channel_id=1, source_target_pairs={{0,1},{1,2},{2,3},{3,4},{4,5},{5,6},{6,7},{7,8},{8,9},{9,10},{10,1... | collective-permute-start | bytes 8257544 | tf_op jit(solution)/shard_map/while/body/eval_jaxpr/ppermute | solution.py:16
  291.8 35.0 %collective-permute-start.1 = (f32[3,4,448,128]{3,2,1,0:T(8,128)}, f32[3,4,448,128]{3,2,1,0:T(8,128)}, u32[]{:S(2)}, u32[]{:S(2)}) collective-permute-start(f32[3,4,448,128]{3,2,1,0:T(8,128)} %get-tuple-element.231), channel_id=1, source_target_pairs={{1,0},{2,1},{3,2},{4,3},{5,4},{6,5},{7,6},{8,7},{9,8},{10,9},{11,1... | collective-permute-start | bytes 8257544 | tf_op jit(solution)/shard_map/while/body/eval_jaxpr/ppermute | solution.py:19
  413.0 5.5 copy-start.2
  500.2 1.3 copy-start
  500.3 1.8 copy-start.1
  505.0 32.2 %collective-permute-start = (f32[3,4,448,128]{3,2,1,0:T(8,128)}, f32[3,4,448,128]{3,2,1,0:T(8,128)}, u32[]{:S(2)}, u32[]{:S(2)}) collective-permute-start(f32[3,4,448,128]{3,2,1,0:T(8,128)} %get-tuple-element.230), channel_id=1, source_target_pairs={{0,1},{1,2},{2,3},{3,4},{4,5},{5,6},{6,7},{7,8},{8,9},{9,10},{10,1... | collective-permute-start | bytes 8257544 | tf_op jit(solution)/shard_map/while/body/eval_jaxpr/ppermute | solution.py:16
  506.9 34.7 %collective-permute-start.1 = (f32[3,4,448,128]{3,2,1,0:T(8,128)}, f32[3,4,448,128]{3,2,1,0:T(8,128)}, u32[]{:S(2)}, u32[]{:S(2)}) collective-permute-start(f32[3,4,448,128]{3,2,1,0:T(8,128)} %get-tuple-element.231), channel_id=1, source_target_pairs={{1,0},{2,1},{3,2},{4,3},{5,4},{6,5},{7,6},{8,7},{9,8},{10,9},{11,1... | collective-permute-start | bytes 8257544 | tf_op jit(solution)/shard_map/while/body/eval_jaxpr/ppermute | solution.py:19
  621.1 0.7 copy-start.7
  621.1 0.7 copy-start.9
  621.1 157.8 %copy-start.5 = (f32[4,8,56,128]{3,2,1,0:T(8,128)S(1)}, f32[4,8,56,128]{3,2,1,0:T(8,128)}, u32[]{:S(2)}) copy-start(f32[4,8,56,128]{3,2,1,0:T(8,128)} %param.7) | copy-start | bytes 2752516
Sparse Core Ops, SparseCore 0:
  621.3 157.6 reduce-scatter.1
